TPU v7x, 32 devices: a whole 2x2x4 slice. The times are simulated.
32 devices in a mesh: group: 1, ctx: 32 (over z, y, x, core).
Axes of the slice: x: 2, y: 2, z: 4, core: 2. Of those that a mesh axis runs over, the one named last changes fastest.
Arguments:
- history: bfloat16 [2, 1024, 8192], P('group', 'ctx'), may hold values from -6 to 6
- lengths: int32 [2], P('group'), may hold values from 256 to 1024
- token_ids: int32 [2, 512], P('group'), may hold values from 0 to 511
- embed: bfloat16 [512, 8192], P('ctx'), may hold values from -6 to 6
- residue: float32 [16, 8192], replicated, may hold values from -0.046875 to 0.046875
- decay: float32 [16, 8192], replicated, may hold values from 0.1 to 400
- skip: float32 [8192], replicated, may hold values from 0.5 to 1.5
Outputs:
- mixed: bfloat16 [2, 512, 8192], P('group', 'ctx')
Inputs may be any that keep to these rules, and one draw needn't show every extreme that they name: `lengths`: history positions at or past a sequence's length are ignored.
All inputs are finite; a program needn't handle non-finite values.
Results may differ from a plain program's by a relative error of at most 0.0005.
Values may be sent and summed in bfloat16 or wider, within the bound.
No kernel may reach another device: no remote copies, remote signals or barrier semaphores. Data moves between devices by JAX's collectives and lax.ppermute only.
A program may use at most 128 MiB of HBM per device.

v0:
```python
import jax
import jax.numpy as jnp
from jax import lax
from jax.experimental import pallas as pl
from jax.experimental.pallas import tpu as pltpu
from jax.sharding import PartitionSpec as P

ROWS = 8
CHUNK = 16
LANES = 128
VMEM = 16 * 2**20
f32 = jnp.float32


def reverse_bits(value, bits):
    result = 0
    for k in range(bits):
        result = result + lax.rem(lax.div(value, 2**k), 2) * 2 ** (bits - 1 - k)
    return result


def merge_rows(parts):
    row = lax.broadcasted_iota(jnp.int32, parts[0].shape, 0)
    low = row < 4
    level = [
        jnp.where(low, parts[i], parts[i + 4]) + pltpu.roll(jnp.where(low, parts[i + 4], parts[i]), 4, 0)
        for i in range(4)
    ]
    for gap in (2, 1):
        first = (row & gap) == 0
        level = [
            jnp.where(first, level[i], level[i + gap])
            + jnp.where(first, pltpu.roll(level[i], 8 - gap, 0), pltpu.roll(level[i + gap], gap, 0))
            for i in range(gap)
        ]
    return level[0]


def fold(x):
    total = x[:ROWS]
    for start in range(ROWS, x.shape[0], ROWS):
        total = total + x[start : start + ROWS]
    return total


def horner(keep, rows_of, count, tile):
    def step(s, sums):
        return tuple(keep * total + rows_of(i, s) for i, total in enumerate(sums))

    return lax.fori_loop(0, tile, step, (jnp.zeros(keep.shape, f32),) * count, unroll=16)


def block_of(me, spot, give, bits):
    core = lax.rem(me, 2)
    top = lax.rem(lax.div(me, 2**bits), 2)
    if give:
        top = 1 - top
    return 2 * (top * 2 ** (bits - 1) + reverse_bits(spot, bits - 1)) + core


def masked(value, length, start):
    row = lax.broadcasted_iota(jnp.int32, value.shape, 0)
    return jnp.where(row < length - start, value.astype(f32), 0.0)


def lift(rate, length, end, tile):
    return jnp.exp(-rate * (jnp.maximum(length - end, -tile) + 1).astype(f32))


def prepare_kernel(
    total_len, bits, lengths_ref, embed_ref, history_ref, decay_ref,
    columns_ref, states_ref, decays_ref, held_ref, ends_ref,
    entries, pieces, wide, lengths, length_sem, load_sem, piece_sem, rate_sem, store_sem,
):
    count, _, block = columns_ref.shape
    half, seqs, tile, _ = pieces.shape
    team = count // 2
    me = lax.axis_index("ctx")

    def fetch(spot, give):
        start = pl.multiple_of(block_of(me, spot, give, bits) * block, block)
        target, index = (pieces, spot) if give else (held_ref, spot + half)
        return (
            pltpu.make_async_copy(decay_ref.at[:, pl.ds(start, block)], decays_ref.at[index], rate_sem.at[index]),
            pltpu.make_async_copy(history_ref.at[:, :, pl.ds(start, block)], target.at[spot], piece_sem.at[index]),
        )

    copies = [copy for give in (True, False) for spot in range(half) for copy in fetch(spot, give)]
    loads = [
        pltpu.make_async_copy(embed_ref.at[:, pl.ds(p * block, block)], entries.at[p], load_sem.at[p])
        for p in range(team)
    ]
    stores = [
        pltpu.make_async_copy(entries, columns_ref.at[pl.ds(h * team, team)], store_sem.at[h]) for h in range(2)
    ]
    length_copy = pltpu.make_async_copy(lengths_ref, lengths, length_sem)
    for copy in [length_copy] + loads + copies:
        copy.start()
    for copy in loads:
        copy.wait()
    for copy in stores:
        copy.start()
    length_copy.wait()
    for b in range(seqs):
        ends_ref[b : b + 1, :] = jnp.full((1, block), lengths[b], jnp.int32)
    for copy in copies[: 2 * half]:
        copy.wait()

    @pl.loop(0, half)
    def _(spot):
        rate = decays_ref[spot] / total_len
        sums = partial_states(rate, lambda b: pieces[spot, b], wide, ends_ref, me * tile)
        for b in range(seqs):
            states_ref[spot, b] = sums[b]

    for copy in copies[2 * half :] + stores:
        copy.wait()


def partial_states(rate, tile_of, wide, ends_ref, start):
    seqs, tile, _ = wide.shape
    keep = jnp.exp(-rate)
    for b in range(seqs):
        wide[b] = masked(tile_of(b), ends_ref[b : b + 1, :], start)
    sums = horner(keep, lambda b, s: wide[b, pl.ds(s, 1), :], seqs, tile)
    return [sums[b] * lift(rate, ends_ref[b : b + 1, :], start + tile, tile) for b in range(seqs)]


def give_kernel(total_len, bits, ends_ref, other_ref, states_ref, decays_ref, out_ref, wide):
    seqs, tile, block = wide.shape
    me = lax.axis_index("ctx")
    partner = me + 1 - 2 * lax.rem(me, 2)

    @pl.loop(0, out_ref.shape[0])
    def _(spot):
        at = pl.ds(pl.multiple_of(block_of(me, spot, True, bits) * block, block), block)
        rate = decays_ref[spot] / total_len
        sums = partial_states(rate, lambda b: other_ref[b, :, at], wide, ends_ref, partner * tile)
        for b in range(seqs):
            out_ref[spot, b] = states_ref[spot, b] + sums[b]


def keep_kernel(total_len, bits, ends_ref, other_ref, held_ref, decays_ref, out_ref, wide):
    seqs, tile, block = wide.shape
    half = out_ref.shape[0]
    me = lax.axis_index("ctx")
    partner = me + 1 - 2 * lax.rem(me, 2)

    @pl.loop(0, half)
    def _(spot):
        at = pl.ds(pl.multiple_of(block_of(me, spot, False, bits) * block, block), block)
        rate = decays_ref[spot + half] / total_len
        own = partial_states(rate, lambda b: held_ref[spot, b], wide, ends_ref, me * tile)
        sums = partial_states(rate, lambda b: other_ref[b, :, at], wide, ends_ref, partner * tile)
        for b in range(seqs):
            out_ref[spot, b] = own[b] + sums[b]


def tables_kernel(total_len, team, span, me_ref, decay_ref, residue_ref, skip_ref, weights_ref, taps_ref, keeps_ref, ages_ref):
    modes, block = decay_ref.shape
    rate = decay_ref[...] / total_len
    residue = residue_ref[...]
    taps = []
    for i in range(CHUNK):
        weight = residue * jnp.exp(-rate * float(i))
        weights_ref[i] = weight
        taps.append(fold(weight))
    for start in range(0, CHUNK, ROWS):
        taps_ref[start : start + ROWS] = merge_rows(taps[start : start + ROWS])
    taps_ref[0:1] = taps_ref[0:1] + skip_ref[...]
    keeps_ref[0] = jnp.exp(-rate)
    keeps_ref[1] = jnp.exp(-rate * float(CHUNK))
    keeps_ref[2] = rate
    chunks = span // CHUNK
    begin = (lax.div(me_ref[0], team) * span).astype(f32)
    times = begin + float(CHUNK) * lax.broadcasted_iota(jnp.int32, (chunks, block), 0).astype(f32)

    @pl.loop(0, modes)
    def _(k):
        ages_ref[k] = jnp.exp(-keeps_ref[2, pl.ds(k, 1), :] * times)


def chunk_rows(group, offset):
    return pl.ds(group * ROWS * CHUNK + offset, ROWS, stride=CHUNK)


def fresh_kernel(team, chosen_ref, table_ref, taps_ref, keeps_ref, conv_ref, carry_ref, fresh, ends):
    seqs, _, _ = chosen_ref.shape
    tiles, span = conv_ref.shape[1:3]
    modes = keeps_ref.shape[1]
    chunks = span // CHUNK
    late = lax.div(lax.axis_index("ctx"), team)
    strips = [(b, t) for t in range(tiles) for b in range(seqs)]

    def look_up(begin):
        for b in range(seqs):
            rows = chosen_ref[b, pl.ds(pl.multiple_of(begin, span), span), :]
            found = jnp.dot(rows, table_ref[...], preferred_element_type=f32)
            for t in range(tiles):
                fresh[b, t] = found[:, t * LANES : (t + 1) * LANES]

    def lanes(t):
        return slice(t * LANES, (t + 1) * LANES)

    def finish_chunks(values, b, t, group):
        for k in range(modes):
            keep = jnp.broadcast_to(keeps_ref[0, k : k + 1, lanes(t)], (ROWS, LANES))
            total = keep * values[0]
            for value in values[1:]:
                total = keep * (total + value)
            ends[b, t, chunk_rows(group, k), :] = total

    def values_of(b, t, group):
        return [fresh[b, t, chunk_rows(group, i), :] for i in range(CHUNK)]

    def rows_of(chunk):
        return pl.ds(pl.multiple_of(chunk * modes, modes), modes)

    for b, t in strips:
        carry_ref[b, t, 0:modes, :] = jnp.zeros((modes, LANES), f32)

    @pl.when(late == 1)
    def _():
        look_up(0)

        @pl.loop(0, chunks // ROWS)
        def _(group):
            for b, t in strips:
                finish_chunks(values_of(b, t, group), b, t, group)

        def advance(chunk, carries):
            return tuple(
                keeps_ref[1, :, lanes(t)] * carry + ends[b, t, rows_of(chunk), :] for (b, t), carry in zip(strips, carries)
            )

        carries = lax.fori_loop(0, chunks, advance, (jnp.zeros((modes, LANES), f32),) * len(strips))
        for (b, t), carry in zip(strips, carries):
            carry_ref[b, t, 0:modes, :] = carry

    look_up(late * span)

    @pl.loop(0, chunks // ROWS)
    def _(group):
        for b, t in strips:
            values = values_of(b, t, group)
            taps = [jnp.broadcast_to(taps_ref[d : d + 1, lanes(t)], (ROWS, LANES)) for d in range(CHUNK)]
            for i in range(CHUNK):
                total = taps[0] * values[i]
                for d in range(1, i + 1):
                    total = total + taps[d] * values[i - d]
                conv_ref[b, t, chunk_rows(group, i), :] = total
            finish_chunks(values, b, t, group)

    @pl.loop(1, chunks)
    def _(chunk):
        for b, t in strips:
            old, new = rows_of(chunk - 1), rows_of(chunk)
            carry_ref[b, t, new, :] = keeps_ref[1, :, lanes(t)] * carry_ref[b, t, old, :] + ends[b, t, old, :]


def mix_kernel(near_ref, far_ref, conv_ref, carry_ref, weights_ref, ages_ref, out_ref, state, total_ref):
    seqs, tiles, span, _ = conv_ref.shape
    modes = near_ref.shape[1]
    chunks = span // CHUNK
    for b in range(seqs):
        state[b] = near_ref[b] + far_ref[b]

    @pl.loop(0, chunks // ROWS)
    def _(group):
        old = pl.ds(pl.multiple_of(group * ROWS, ROWS), ROWS)
        for t in range(tiles):
            at = slice(t * LANES, (t + 1) * LANES)
            begun = [
                [
                    carry_ref[b, t, chunk_rows(group, k), :] + ages_ref[k, old, at] * state[b, k : k + 1, at]
                    for k in range(modes)
                ]
                for b in range(seqs)
            ]
            for i in range(CHUNK):
                weights = [weights_ref[i, k : k + 1, at] for k in range(modes)]
                for b in range(seqs):
                    total = conv_ref[b, t, chunk_rows(group, i), :]
                    other = weights[0] * begun[b][0]
                    for k in range(1, modes):
                        if k % 2:
                            total = total + weights[k] * begun[b][k]
                        else:
                            other = other + weights[k] * begun[b][k]
                    total_ref[b, t, chunk_rows(0, i), :] = total + other
        for chunk in range(ROWS):
            first = pl.multiple_of((group * ROWS + chunk) * CHUNK, CHUNK)
            for b, t in ((b, t) for b in range(seqs) for t in range(tiles)):
                at = slice(t * LANES, (t + 1) * LANES)
                mixed = total_ref[b, t, chunk * CHUNK : (chunk + 1) * CHUNK, :].astype(jnp.bfloat16)
                if len(out_ref.shape) == 4:
                    own = out_ref.shape[2]
                    spot = pl.ds(pl.multiple_of(lax.rem(first, own), CHUNK), CHUNK)
                    out_ref[lax.div(first, own), b, spot, at] = mixed
                else:
                    out_ref[b, pl.ds(first, CHUNK), at] = mixed


def join_kernel(mixed_ref, out_ref, sem):
    count, _, _, block = mixed_ref.shape
    copies = [
        pltpu.make_async_copy(mixed_ref.at[p], out_ref.at[:, :, pl.ds(p * block, block)], sem.at[p])
        for p in range(count)
    ]
    for copy in copies:
        copy.start()
    for copy in copies:
        copy.wait()


def call(kernel, grid, scalars, in_specs, out_specs, out_shape, flops, moved, scratch=()):
    return pl.pallas_call(
        kernel,
        grid_spec=pltpu.PrefetchScalarGridSpec(
            num_scalar_prefetch=scalars,
            grid=grid,
            in_specs=in_specs,
            out_specs=out_specs,
            scratch_shapes=scratch,
        ),
        out_shape=out_shape,
        cost_estimate=pl.CostEstimate(flops=flops, bytes_accessed=moved, transcendentals=0),
        compiler_params=pltpu.CompilerParams(vmem_limit_bytes=VMEM),
    )


def body(history, lengths, token_ids, embed, residue, decay, skip):
    devices = lax.axis_size("ctx")
    me = lax.axis_index("ctx")
    seqs, tile, width = history.shape
    modes = decay.shape[0]
    rows = embed.shape[0]
    gen = token_ids.shape[1]
    total_len = float(tile * devices)
    team = devices // 2
    chips = team // 2
    bits = chips.bit_length() - 1
    assert devices == 4 * 2**bits
    block = width // team
    span = gen // 2
    chunks = span // CHUNK
    tiles = block // LANES
    assert block % LANES == 0 and span % (ROWS * CHUNK) == 0
    own = gen // devices
    place = me.astype(jnp.int32).reshape(1)
    history, embed, residue, decay, skip, lengths = (
        pltpu.with_memory_space_constraint(x, pltpu.HBM)
        for x in (history, embed, residue, decay, skip.reshape(1, width), lengths)
    )
    chip = lax.rem(me, team) // 2
    opposite = [(j, (j + team) % devices) for j in range(devices)]
    shape = jax.ShapeDtypeStruct

    def paired(x, distance):
        return lax.ppermute(x, "ctx", [(j, j ^ distance) for j in range(devices)])

    swapped = pltpu.with_memory_space_constraint(paired(history, 1), pltpu.VMEM)

    hbm = pl.BlockSpec(memory_space=pltpu.HBM)
    vmem = pl.BlockSpec(memory_space=pltpu.VMEM)
    half = chips // 2
    columns, states, decays, held, ends = call(
        lambda *refs: prepare_kernel(total_len, bits, *refs),
        (1,),
        0,
        [hbm] * 4,
        [hbm, vmem, vmem, vmem, vmem],
        [
            shape((devices, rows, block), jnp.bfloat16),
            shape((half, seqs, modes, block), f32),
            shape((chips, modes, block), f32),
            shape((half, seqs, tile, block), jnp.bfloat16),
            shape((seqs, block), jnp.int32),
        ],
        2 * seqs * tile * modes * block * half,
        2**20,
        [
            pltpu.VMEM((team, rows, block), jnp.bfloat16),
            pltpu.VMEM((half, seqs, tile, block), jnp.bfloat16),
            pltpu.VMEM((seqs, tile, block), f32),
            pltpu.SMEM((seqs,), jnp.int32),
            pltpu.SemaphoreType.DMA(()),
            pltpu.SemaphoreType.DMA((team,)),
            pltpu.SemaphoreType.DMA((chips,)),
            pltpu.SemaphoreType.DMA((chips,)),
            pltpu.SemaphoreType.DMA((2,)),
        ],
    )(lengths, embed, history, decay)
    table = lax.all_to_all(columns, "ctx", 0, 0, tiled=True)
    table = table.reshape(devices * rows, block)

    def finish(kernel, operand, flops):
        return call(
            lambda *refs: kernel(total_len, bits, *refs),
            (1,),
            0,
            [vmem] * 4,
            vmem,
            shape((half, seqs, modes, block), f32),
            flops,
            2**20,
            [pltpu.VMEM((seqs, tile, block), f32)],
        )(ends, swapped, operand, decays)

    work = 2 * seqs * tile * modes * block * half
    sent = finish(give_kernel, states, work)
    came = paired(sent, 2**bits)
    mine = finish(keep_kernel, held, 2 * work) + came
    done = 0
    while done < bits - 1:
        now = min(2, bits - 1 - done)
        ways, size = 2**now, mine.shape[0] // 2**now
        digit = lax.rem(lax.div(chip, 2**done), ways)
        take = lambda x, d: lax.dynamic_slice_in_dim(x, reverse_bits(d, now) * size, size, 0)
        total = take(mine, digit)
        for d in range(ways - 1, 0, -1):
            flipped = digit ^ d
            total = total + paired(take(mine, flipped), d << (done + 1))
        mine = total
        done += now
    near = mine[0]
    far = lax.ppermute(near, "ctx", opposite)

    entry = lax.broadcasted_iota(jnp.int32, (seqs, gen, devices * rows), 2)
    chosen = (token_ids[:, :, None] == entry).astype(jnp.bfloat16)
    strip = lambda g, at: (0, lax.rem(at[0], team))
    weights, taps, keeps, ages = call(
        lambda *refs: tables_kernel(total_len, team, span, *refs),
        (1,),
        1,
        [pl.BlockSpec((modes, block), strip)] * 2 + [pl.BlockSpec((1, block), strip)],
        [vmem] * 4,
        [
            shape((CHUNK, modes, block), f32),
            shape((CHUNK, block), f32),
            shape((3, modes, block), f32),
            shape((modes, chunks, block), f32),
        ],
        10**6,
        2**20,
    )(place, decay, residue, skip)
    conv, carry = call(
        lambda *refs: fresh_kernel(team, *refs),
        (1,),
        0,
        [vmem] * 4,
        [vmem] * 2,
        [shape((seqs, tiles, span, LANES), f32), shape((seqs, tiles, chunks * modes, LANES), f32)],
        6 * seqs * span * modes * block,
        2**21,
        [pltpu.VMEM((seqs, tiles, span, LANES), f32), pltpu.VMEM((seqs, tiles, chunks * modes, LANES), f32)],
    )(chosen, table, taps, keeps)

    direct = own % CHUNK == 0
    mixed = call(
        mix_kernel,
        (1,),
        0,
        [vmem] * 6,
        vmem,
        shape((team, seqs, own, block) if direct else (seqs, span, block), jnp.bfloat16),
        3 * seqs * span * modes * block,
        2**21,
        [pltpu.VMEM((seqs, modes, block), f32), pltpu.VMEM((seqs, tiles, ROWS * CHUNK, LANES), f32)],
    )(near, far, conv, carry, weights, ages)
    if not direct:
        mixed = mixed.reshape(seqs, team, own, block).transpose(1, 0, 2, 3)
    halves = [[h * team + p for p in range(team)] for h in range(2)]
    result = lax.all_to_all(mixed, "ctx", 0, 0, tiled=True, axis_index_groups=halves)
    return call(
        join_kernel,
        (1,),
        0,
        [vmem],
        hbm,
        shape((seqs, own, width), jnp.bfloat16),
        10**5,
        2**20,
        [pltpu.SemaphoreType.DMA((team,))],
    )(result)


def solution(mesh):
    placed = (P("group", "ctx", None), P("group"), P("group", None), P("ctx", None), P(), P(), P())
    return jax.shard_map(body, mesh=mesh, in_specs=placed, out_specs=P("group", "ctx", None), check_vma=False)
```

profile of v0, /device:TPU:0, one launch (start us, length us, event | category | flops | bytes accessed | tf_op | source)
XLA Modules:
  0.0 56.3 jit_solution(12721937653761433686)
XLA Ops:
  0.0 0.5 collective-permute-start
  0.5 2.3 %shard_map.73 = (bf16[32,16,512]{2,1,0:T(8,128)(2,1)}, f32[4,2,16,512]{3,2,1,0:T(8,128)S(1)}, f32[8,16,512]{2,1,0:T(8,128)S(1)}, bf16[4,2,32,512]{3,2,1,0:T(8,128)(2,1)S(1)}, s32[2,512]{1,0:T(2,128)S(1)}) custom-call(s32[2]{0:T(128)} %refs_0_.1, bf16[16,8192]{1,0:T(8,128)(2,1)} %refs_1_.2, bf16[2,32,8192]{2,1,0:T(8,128)(2,1)} %refs_2_.2, f32[16,8192]{1,0:T(8,128)} %refs_1_.3), custom_call_target="tpu_custom_call" | custom-call | flops 4194304 | bytes 1048576 | tf_op jit(solution)/shard_map/pallas_call | solution.py:367
  2.8 7.0 %all-to-all-start = ((bf16[32,16,512]{2,1,0:T(8,128)(2,1)}), bf16[32,16,512]{2,1,0:T(8,128)(2,1)S(1)}, u32[]{:S(2)}, u32[]{:S(2)}) async-start(bf16[32,16,512]{2,1,0:T(8,128)(2,1)} %get-tuple-element.20), calls=%async_computation | async-start | bytes 1048576 | tf_op jit(solution)/shard_map/all_to_all | solution.py:394
  9.7 0.0 collective-permute-done.refs_1_
  9.7 0.8 %shard_map.75 = f32[4,2,16,512]{3,2,1,0:T(8,128)S(1)} custom-call(s32[2,512]{1,0:T(2,128)S(1)} %get-tuple-element.16.refs_0_, bf16[2,32,8192]{2,1,0:T(8,128)(2,1)S(1)} %collective-permute-done.refs_1_, f32[4,2,16,512]{3,2,1,0:T(8,128)S(1)} %get-tuple-element.19.refs_2_, f32[8,16,512]{2,1,0:T(8,128)S(1)} %get-tuple-element.18.refs_3_), custom_call_target="tpu_custom_call" | custom-call | flops 4194304 | bytes 1048576 | tf_op jit(solution)/shard_map/pallas_call | solution.py:398
  10.5 1.8 %collective-permute-start.1 = (f32[4,2,16,512]{3,2,1,0:T(8,128)S(1)}, f32[4,2,16,512]{3,2,1,0:T(8,128)S(1)}, u32[]{:S(2)}, u32[]{:S(2)}) collective-permute-start(f32[4,2,16,512]{3,2,1,0:T(8,128)S(1)} %shard_map.75), channel_id=1, source_target_pairs={{0,8},{1,9},{2,10},{3,11},{4,12},{5,13},{6,14},{7,15},{8,0},{9,1},... | collective-permute-start | bytes 786440 | tf_op jit(solution)/shard_map/ppermute | solution.py:360
  12.4 1.5 %shard_map.74 = f32[4,2,16,512]{3,2,1,0:T(8,128)S(1)} custom-call(s32[2,512]{1,0:T(2,128)S(1)} %get-tuple-element.16.refs_0_, bf16[2,32,8192]{2,1,0:T(8,128)(2,1)S(1)} %collective-permute-done.refs_1_, bf16[4,2,32,512]{3,2,1,0:T(8,128)(2,1)S(1)} %get-tuple-element.17.refs_2_, f32[8,16,512]{2,1,0:T(8,128)S(1)} %get-tuple-element.18.refs_3_), custom_call_target="tpu_custom_call" | custom-call | flops 8388608 | bytes 1048576 | tf_op jit(solution)/shard_map/pallas_call | solution.py:398
  13.9 0.0 copy-start
  13.9 12.7 %collective-permute-done.1 = f32[4,2,16,512]{3,2,1,0:T(8,128)S(1)} collective-permute-done((f32[4,2,16,512]{3,2,1,0:T(8,128)S(1)}, f32[4,2,16,512]{3,2,1,0:T(8,128)S(1)}, u32[]{:S(2)}, u32[]{:S(2)}) %collective-permute-start.1) | collective-permute-done | bytes 262176 | tf_op jit(solution)/shard_map/ppermute | solution.py:360
  26.7 2.4 %collective-permute-start.2 = (f32[1,2,16,512]{3,2,1,0:T(8,128)S(1)}, f32[1,2,16,512]{3,2,1,0:T(8,128)S(1)}, u32[]{:S(2)}, u32[]{:S(2)}) collective-permute-start(f32[1,2,16,512]{3,2,1,0:T(8,128)S(1)} %get-tuple-element.27), channel_id=1, source_target_pairs={{0,6},{1,7},{2,4},{3,5},{4,2},{5,3},{6,0},{7,1},{8,14},{9,15},{10,... | collective-permute-start | bytes 196616 | tf_op jit(solution)/shard_map/ppermute | solution.py:360
  29.1 0.6 collective-permute-start.4
  29.7 0.6 collective-permute-start.3
  30.2 2.2 %collective-permute-done.2 = f32[1,2,16,512]{3,2,1,0:T(8,128)S(1)} collective-permute-done((f32[1,2,16,512]{3,2,1,0:T(8,128)S(1)}, f32[1,2,16,512]{3,2,1,0:T(8,128)S(1)}, u32[]{:S(2)}, u32[]{:S(2)}) %collective-permute-start.2) | collective-permute-done | bytes 65568 | tf_op jit(solution)/shard_map/ppermute | solution.py:360
  32.5 0.9 %collective-permute-done.4 = f32[1,2,16,512]{3,2,1,0:T(8,128)S(1)} collective-permute-done((f32[1,2,16,512]{3,2,1,0:T(8,128)S(1)}, f32[1,2,16,512]{3,2,1,0:T(8,128)S(1)}, u32[]{:S(2)}, u32[]{:S(2)}) %collective-permute-start.4) | collective-permute-done | bytes 65568 | tf_op jit(solution)/shard_map/ppermute | solution.py:360
  33.4 0.6 collective-permute-done.3
  34.0 2.5 %collective-permute-start.5 = (f32[2,16,512]{2,1,0:T(8,128)S(1)}, f32[2,16,512]{2,1,0:T(8,128)S(1)}, u32[]{:S(2)}, u32[]{:S(2)}) collective-permute-start(f32[2,16,512]{2,1,0:T(8,128)S(1)} %add_bitcast_fusion.near_ref), channel_id=1, source_target_pairs={{0,16},{1,17},{2,18},{3,19},{4,20},{5,21},{6,22},{7,23},{8,24},{9,... | collective-permute-start | bytes 196616 | tf_op jit(solution)/shard_map/ppermute | solution.py:427
  36.5 0.0 copy-done
  36.5 0.2 fusion.refs_0_
  36.7 1.2 %shard_map.76 = (f32[16,16,512]{2,1,0:T(8,128)S(1)}, f32[16,512]{1,0:T(8,128)S(1)}, f32[3,16,512]{2,1,0:T(8,128)S(1)}, f32[16,16,512]{2,1,0:T(8,128)S(1)}) custom-call(s32[1]{0:T(128)} %bitcast.2.refs_0_, f32[16,8192]{1,0:T(8,128)} %refs_1_.3, f32[16,8192]{1,0:T(8,128)} %refs_2_.3, f32[1,8192]{1,0:T(1,128)} %bitcast.6), custom_call_target="tpu_custom_call" | custom-call | flops 1000000 | bytes 1048576 | tf_op jit(solution)/shard_map/pallas_call | solution.py:432
  37.9 0.0 all-to-all-done
  37.9 2.5 %shard_map.77 = (f32[2,4,256,128]{3,2,1,0:T(8,128)S(1)}, f32[2,4,256,128]{3,2,1,0:T(8,128)S(1)}) custom-call(bf16[2,512,512]{2,1,0:T(8,128)(2,1)S(1)} %fusion.refs_0_, bf16[512,512]{1,0:T(8,128)(2,1)S(1)} %bitcast.5, f32[16,512]{1,0:T(8,128)S(1)} %get-tuple-element.21.refs_2_, f32[3,16,512]{2,1,0:T(8,128)S(1)} %get-tuple-element.22.refs_3_), custom_call_target="tpu_custom_call" | custom-call | flops 25165824 | bytes 2097152 | tf_op jit(solution)/shard_map/pallas_call | solution.py:447
  40.4 0.0 collective-permute-done.5.far_ref
  40.4 1.8 %shard_map.78 = bf16[16,2,16,512]{3,2,1,0:T(8,128)(2,1)S(1)} custom-call(f32[2,16,512]{2,1,0:T(8,128)S(1)} %add_bitcast_fusion.near_ref, f32[2,16,512]{2,1,0:T(8,128)S(1)} %collective-permute-done.5.far_ref, f32[2,4,256,128]{3,2,1,0:T(8,128)S(1)} %get-tuple-element.23.conv_ref, f32[2,4,256,128]{3,2,1,0:T(8,128)S(1)} %get-tuple-element.24.carry_ref, ...), custom_call_target="tpu_custom_call" | custom-call | flops 12582912 | bytes 2097152 | tf_op jit(solution)/shard_map/pallas_call | solution.py:460
  42.2 13.2 %all_to_all.10.mixed_ref = bf16[16,2,16,512]{3,2,1,0:T(8,128)(2,1)S(1)} all-to-all(bf16[16,2,16,512]{3,2,1,0:T(8,128)(2,1)S(1)} %shard_map.78), channel_id=1, replica_groups={{0,1,2,3,4,5,6,7,8,9,10,11,12,13,14,15},{16,17,18,19,20,21,22,23,24,25,..., dimensions={0} | all-to-all | bytes 1048576 | tf_op jit(solution)/shard_map/all_to_all | solution.py:474
  55.4 0.9 %shard_map.79 = bf16[2,16,8192]{2,1,0:T(8,128)(2,1)} custom-call(bf16[16,2,16,512]{3,2,1,0:T(8,128)(2,1)S(1)} %all_to_all.10.mixed_ref), custom_call_target="tpu_custom_call" | custom-call | flops 100000 | bytes 1048576 | tf_op jit(solution)/shard_map/pallas_call | solution.py:475
  (3 shorter events, 0.1 us)
Async XLA Ops:
  0.0 9.7 %collective-permute-start = (bf16[2,32,8192]{2,1,0:T(8,128)(2,1)}, bf16[2,32,8192]{2,1,0:T(8,128)(2,1)S(1)}, u32[]{:S(2)}, u32[]{:S(2)}) collective-permute-start(bf16[2,32,8192]{2,1,0:T(8,128)(2,1)} %refs_2_.2), channel_id=1, source_target_pairs={{0,1},{1,0},{2,3},{3,2},{4,5},{5,4},{6,7},{7,6},{8,9},{9,8},{10,11... | collective-permute-start | bytes 3145736 | tf_op jit(solution)/shard_map/ppermute | solution.py:360
  2.8 35.1 %all-to-all-start = ((bf16[32,16,512]{2,1,0:T(8,128)(2,1)}), bf16[32,16,512]{2,1,0:T(8,128)(2,1)S(1)}, u32[]{:S(2)}, u32[]{:S(2)}) async-start(bf16[32,16,512]{2,1,0:T(8,128)(2,1)} %get-tuple-element.20), calls=%async_computation | async-start | bytes 1048576 | tf_op jit(solution)/shard_map/all_to_all | solution.py:394
  10.5 16.1 %collective-permute-start.1 = (f32[4,2,16,512]{3,2,1,0:T(8,128)S(1)}, f32[4,2,16,512]{3,2,1,0:T(8,128)S(1)}, u32[]{:S(2)}, u32[]{:S(2)}) collective-permute-start(f32[4,2,16,512]{3,2,1,0:T(8,128)S(1)} %shard_map.75), channel_id=1, source_target_pairs={{0,8},{1,9},{2,10},{3,11},{4,12},{5,13},{6,14},{7,15},{8,0},{9,1},... | collective-permute-start | bytes 786440 | tf_op jit(solution)/shard_map/ppermute | solution.py:360
  13.9 22.6 %copy-start = (s32[2,512]{1,0:T(2,128)S(1)}, s32[2,512]{1,0:T(2,128)}, u32[]{:S(2)}) copy-start(s32[2,512]{1,0:T(2,128)} %param.9) | copy-start | bytes 12292
  26.7 5.8 %collective-permute-start.2 = (f32[1,2,16,512]{3,2,1,0:T(8,128)S(1)}, f32[1,2,16,512]{3,2,1,0:T(8,128)S(1)}, u32[]{:S(2)}, u32[]{:S(2)}) collective-permute-start(f32[1,2,16,512]{3,2,1,0:T(8,128)S(1)} %get-tuple-element.27), channel_id=1, source_target_pairs={{0,6},{1,7},{2,4},{3,5},{4,2},{5,3},{6,0},{7,1},{8,14},{9,15},{10,... | collective-permute-start | bytes 196616 | tf_op jit(solution)/shard_map/ppermute | solution.py:360
  29.1 4.3 %collective-permute-start.4 = (f32[1,2,16,512]{3,2,1,0:T(8,128)S(1)}, f32[1,2,16,512]{3,2,1,0:T(8,128)S(1)}, u32[]{:S(2)}, u32[]{:S(2)}) collective-permute-start(f32[1,2,16,512]{3,2,1,0:T(8,128)S(1)} %get-tuple-element.28), channel_id=1, source_target_pairs={{0,2},{1,3},{2,0},{3,1},{4,6},{5,7},{6,4},{7,5},{8,10},{9,11},{10,... | collective-permute-start | bytes 196616 | tf_op jit(solution)/shard_map/ppermute | solution.py:360
  29.7 4.3 %collective-permute-start.3 = (f32[1,2,16,512]{3,2,1,0:T(8,128)S(1)}, f32[1,2,16,512]{3,2,1,0:T(8,128)S(1)}, u32[]{:S(2)}, u32[]{:S(2)}) collective-permute-start(f32[1,2,16,512]{3,2,1,0:T(8,128)S(1)} %get-tuple-element.29), channel_id=1, source_target_pairs={{0,4},{1,5},{2,6},{3,7},{4,0},{5,1},{6,2},{7,3},{8,12},{9,13},{10,... | collective-permute-start | bytes 196616 | tf_op jit(solution)/shard_map/ppermute | solution.py:360
  34.0 6.5 %collective-permute-start.5 = (f32[2,16,512]{2,1,0:T(8,128)S(1)}, f32[2,16,512]{2,1,0:T(8,128)S(1)}, u32[]{:S(2)}, u32[]{:S(2)}) collective-permute-start(f32[2,16,512]{2,1,0:T(8,128)S(1)} %add_bitcast_fusion.near_ref), channel_id=1, source_target_pairs={{0,16},{1,17},{2,18},{3,19},{4,20},{5,21},{6,22},{7,23},{8,24},{9,... | collective-permute-start | bytes 196616 | tf_op jit(solution)/shard_map/ppermute | solution.py:427
where the time goes:
time: 56.6 us; the launch traced here: 56.3 us
  waiting for transfers between devices  16.4 us (29%)
  starting transfers between devices  15.4 us (27%)
  blocking collectives  13.2 us (23%)
  Pallas kernels  10.9 us (19%)
    ppermute x5, waiting for transfers between devices, paired(): return lax.ppermute(x, 'ctx', [(j, j ^ distance) for j in range(devices)])  16.4 us
    all_to_all x1, blocking collectives, body(): lax.all_to_all(mixed, 'ctx', 0, 0, tiled=True, axis_index_groups=halves)  13.2 us
    all_to_all x1, starting transfers between devices, body(): table = lax.all_to_all(columns, 'ctx', 0, 0, tiled=True)  6.95 us
    ppermute x5, starting transfers between devices, paired(): return lax.ppermute(x, 'ctx', [(j, j ^ distance) for j in range(devices)])  5.88 us
    ppermute x1, starting transfers between devices, body(): far = lax.ppermute(near, 'ctx', opposite)  2.52 us
    pallas_call x1, Pallas kernels, body(): call(lambda *refs: fresh_kernel(team, *refs), (1,), 0, [vmem] * 4, [vmem]...  2.51 us
    pallas_call x2, Pallas kernels, finish(): call(lambda *refs: kernel(total_len, bits, *refs), (1,), 0, [vmem] * 4, v...  2.28 us
    pallas_call x1, Pallas kernels, body(): call(lambda *refs: prepare_kernel(total_len, bits, *refs), (1,), 0, [hbm]...  2.27 us
  transfers between devices with their start and end apart: 7, of which 4 were waited for; matrix products, arithmetic and copies ran while one was open for 1% of the time, Pallas kernels for 15%

commit v1 on v0

--- a/solution.py
+++ b/solution.py
@@ -47,7 +47,7 @@
     def step(s, sums):
         return tuple(keep * total + rows_of(i, s) for i, total in enumerate(sums))
 
-    return lax.fori_loop(0, tile, step, (jnp.zeros(keep.shape, f32),) * count, unroll=16)
+    return lax.fori_loop(0, tile, step, (jnp.zeros(keep.shape, f32),) * count, unroll=True)
 
 
 def block_of(me, spot, give, bits):
@@ -233,7 +233,7 @@
                 keeps_ref[1, :, lanes(t)] * carry + ends[b, t, rows_of(chunk), :] for (b, t), carry in zip(strips, carries)
             )
 
-        carries = lax.fori_loop(0, chunks, advance, (jnp.zeros((modes, LANES), f32),) * len(strips))
+        carries = lax.fori_loop(0, chunks, advance, (jnp.zeros((modes, LANES), f32),) * len(strips), unroll=4)
         for (b, t), carry in zip(strips, carries):
             carry_ref[b, t, 0:modes, :] = carry
 
@@ -251,11 +251,16 @@
                 conv_ref[b, t, chunk_rows(group, i), :] = total
             finish_chunks(values, b, t, group)
 
-    @pl.loop(1, chunks)
-    def _(chunk):
-        for b, t in strips:
-            old, new = rows_of(chunk - 1), rows_of(chunk)
-            carry_ref[b, t, new, :] = keeps_ref[1, :, lanes(t)] * carry_ref[b, t, old, :] + ends[b, t, old, :]
+    def settle(chunk, carries):
+        settled = []
+        for (b, t), carry in zip(strips, carries):
+            carry = keeps_ref[1, :, lanes(t)] * carry + ends[b, t, rows_of(chunk), :]
+            carry_ref[b, t, rows_of(chunk + 1), :] = carry
+            settled.append(carry)
+        return tuple(settled)
+
+    begun = tuple(carry_ref[b, t, 0:modes, :] for b, t in strips)
+    lax.fori_loop(0, chunks - 1, settle, begun, unroll=5)
 
 
 def mix_kernel(near_ref, far_ref, conv_ref, carry_ref, weights_ref, ages_ref, out_ref, state, total_ref):

time: 56.6 us -> 56.5 us (level)
  transfers between devices with their start and end apart: 7 -> 7, of which waited for: 4 -> 4; matrix products, arithmetic and copies ran while one was open for 1% -> 1% of each run, Pallas kernels for 15% -> 14%
where the time goes in v1:
time: 56.5 us; the launch traced here: 56.2 us
  waiting for transfers between devices  16.6 us (29%)
  starting transfers between devices  15.4 us (27%)
  blocking collectives  13.2 us (23%)
  Pallas kernels  10.6 us (19%)
    ppermute x5, waiting for transfers between devices, paired(): return lax.ppermute(x, 'ctx', [(j, j ^ distance) for j in range(devices)])  16.6 us
    all_to_all x1, blocking collectives, body(): lax.all_to_all(mixed, 'ctx', 0, 0, tiled=True, axis_index_groups=halves)  13.2 us
    all_to_all x1, starting transfers between devices, body(): table = lax.all_to_all(columns, 'ctx', 0, 0, tiled=True)  6.95 us
    ppermute x5, starting transfers between devices, paired(): return lax.ppermute(x, 'ctx', [(j, j ^ distance) for j in range(devices)])  5.88 us
    ppermute x1, starting transfers between devices, body(): far = lax.ppermute(near, 'ctx', opposite)  2.52 us
    pallas_call x1, Pallas kernels, body(): call(lambda *refs: fresh_kernel(team, *refs), (1,), 0, [vmem] * 4, [vmem]...  2.39 us
    pallas_call x1, Pallas kernels, body(): call(lambda *refs: prepare_kernel(total_len, bits, *refs), (1,), 0, [hbm]...  2.26 us
    pallas_call x2, Pallas kernels, finish(): call(lambda *refs: kernel(total_len, bits, *refs), (1,), 0, [vmem] * 4, v...  2.09 us
  transfers between devices with their start and end apart: 7, of which 4 were waited for; matrix products, arithmetic and copies ran while one was open for 1% of the time, Pallas kernels for 14%

profile of v1, /device:TPU:0, one launch (start us, length us, event | category | flops | bytes accessed | tf_op | source)
XLA Modules:
  0.0 56.2 jit_solution(10390086079344223516)
XLA Ops:
  0.0 0.5 collective-permute-start
  0.5 2.3 %shard_map.73 = (bf16[32,16,512]{2,1,0:T(8,128)(2,1)}, f32[4,2,16,512]{3,2,1,0:T(8,128)S(1)}, f32[8,16,512]{2,1,0:T(8,128)S(1)}, bf16[4,2,32,512]{3,2,1,0:T(8,128)(2,1)S(1)}, s32[2,512]{1,0:T(2,128)S(1)}) custom-call(s32[2]{0:T(128)} %refs_0_.1, bf16[16,8192]{1,0:T(8,128)(2,1)} %refs_1_.2, bf16[2,32,8192]{2,1,0:T(8,128)(2,1)} %refs_2_.2, f32[16,8192]{1,0:T(8,128)} %refs_1_.3), custom_call_target="tpu_custom_call" | custom-call | flops 4194304 | bytes 1048576 | tf_op jit(solution)/shard_map/pallas_call | solution.py:372
  2.8 7.0 %all-to-all-start = ((bf16[32,16,512]{2,1,0:T(8,128)(2,1)}), bf16[32,16,512]{2,1,0:T(8,128)(2,1)S(1)}, u32[]{:S(2)}, u32[]{:S(2)}) async-start(bf16[32,16,512]{2,1,0:T(8,128)(2,1)} %get-tuple-element.20), calls=%async_computation | async-start | bytes 1048576 | tf_op jit(solution)/shard_map/all_to_all | solution.py:399
  9.7 0.0 collective-permute-done.refs_1_
  9.7 0.7 %shard_map.75 = f32[4,2,16,512]{3,2,1,0:T(8,128)S(1)} custom-call(s32[2,512]{1,0:T(2,128)S(1)} %get-tuple-element.16.refs_0_, bf16[2,32,8192]{2,1,0:T(8,128)(2,1)S(1)} %collective-permute-done.refs_1_, f32[4,2,16,512]{3,2,1,0:T(8,128)S(1)} %get-tuple-element.19.refs_2_, f32[8,16,512]{2,1,0:T(8,128)S(1)} %get-tuple-element.18.refs_3_), custom_call_target="tpu_custom_call" | custom-call | flops 4194304 | bytes 1048576 | tf_op jit(solution)/shard_map/pallas_call | solution.py:403
  10.5 1.8 %collective-permute-start.1 = (f32[4,2,16,512]{3,2,1,0:T(8,128)S(1)}, f32[4,2,16,512]{3,2,1,0:T(8,128)S(1)}, u32[]{:S(2)}, u32[]{:S(2)}) collective-permute-start(f32[4,2,16,512]{3,2,1,0:T(8,128)S(1)} %shard_map.75), channel_id=1, source_target_pairs={{0,8},{1,9},{2,10},{3,11},{4,12},{5,13},{6,14},{7,15},{8,0},{9,1},... | collective-permute-start | bytes 786440 | tf_op jit(solution)/shard_map/ppermute | solution.py:365
  12.3 1.4 %shard_map.74 = f32[4,2,16,512]{3,2,1,0:T(8,128)S(1)} custom-call(s32[2,512]{1,0:T(2,128)S(1)} %get-tuple-element.16.refs_0_, bf16[2,32,8192]{2,1,0:T(8,128)(2,1)S(1)} %collective-permute-done.refs_1_, bf16[4,2,32,512]{3,2,1,0:T(8,128)(2,1)S(1)} %get-tuple-element.17.refs_2_, f32[8,16,512]{2,1,0:T(8,128)S(1)} %get-tuple-element.18.refs_3_), custom_call_target="tpu_custom_call" | custom-call | flops 8388608 | bytes 1048576 | tf_op jit(solution)/shard_map/pallas_call | solution.py:403
  13.7 0.0 copy-start
  13.7 12.9 %collective-permute-done.1 = f32[4,2,16,512]{3,2,1,0:T(8,128)S(1)} collective-permute-done((f32[4,2,16,512]{3,2,1,0:T(8,128)S(1)}, f32[4,2,16,512]{3,2,1,0:T(8,128)S(1)}, u32[]{:S(2)}, u32[]{:S(2)}) %collective-permute-start.1) | collective-permute-done | bytes 262176 | tf_op jit(solution)/shard_map/ppermute | solution.py:365
  26.7 2.4 %collective-permute-start.2 = (f32[1,2,16,512]{3,2,1,0:T(8,128)S(1)}, f32[1,2,16,512]{3,2,1,0:T(8,128)S(1)}, u32[]{:S(2)}, u32[]{:S(2)}) collective-permute-start(f32[1,2,16,512]{3,2,1,0:T(8,128)S(1)} %get-tuple-element.27), channel_id=1, source_target_pairs={{0,6},{1,7},{2,4},{3,5},{4,2},{5,3},{6,0},{7,1},{8,14},{9,15},{10,... | collective-permute-start | bytes 196616 | tf_op jit(solution)/shard_map/ppermute | solution.py:365
  29.1 0.6 %collective-permute-start.4 = (f32[1,2,16,512]{3,2,1,0:T(8,128)S(1)}, f32[1,2,16,512]{3,2,1,0:T(8,128)S(1)}, u32[]{:S(2)}, u32[]{:S(2)}) collective-permute-start(f32[1,2,16,512]{3,2,1,0:T(8,128)S(1)} %get-tuple-element.28), channel_id=1, source_target_pairs={{0,2},{1,3},{2,0},{3,1},{4,6},{5,7},{6,4},{7,5},{8,10},{9,11},{10,... | collective-permute-start | bytes 196616 | tf_op jit(solution)/shard_map/ppermute | solution.py:365
  29.7 0.6 collective-permute-start.3
  30.2 2.2 %collective-permute-done.2 = f32[1,2,16,512]{3,2,1,0:T(8,128)S(1)} collective-permute-done((f32[1,2,16,512]{3,2,1,0:T(8,128)S(1)}, f32[1,2,16,512]{3,2,1,0:T(8,128)S(1)}, u32[]{:S(2)}, u32[]{:S(2)}) %collective-permute-start.2) | collective-permute-done | bytes 65568 | tf_op jit(solution)/shard_map/ppermute | solution.py:365
  32.5 0.9 %collective-permute-done.4 = f32[1,2,16,512]{3,2,1,0:T(8,128)S(1)} collective-permute-done((f32[1,2,16,512]{3,2,1,0:T(8,128)S(1)}, f32[1,2,16,512]{3,2,1,0:T(8,128)S(1)}, u32[]{:S(2)}, u32[]{:S(2)}) %collective-permute-start.4) | collective-permute-done | bytes 65568 | tf_op jit(solution)/shard_map/ppermute | solution.py:365
  33.4 0.6 %collective-permute-done.3 = f32[1,2,16,512]{3,2,1,0:T(8,128)S(1)} collective-permute-done((f32[1,2,16,512]{3,2,1,0:T(8,128)S(1)}, f32[1,2,16,512]{3,2,1,0:T(8,128)S(1)}, u32[]{:S(2)}, u32[]{:S(2)}) %collective-permute-start.3) | collective-permute-done | bytes 65568 | tf_op jit(solution)/shard_map/ppermute | solution.py:365
  34.0 2.5 %collective-permute-start.5 = (f32[2,16,512]{2,1,0:T(8,128)S(1)}, f32[2,16,512]{2,1,0:T(8,128)S(1)}, u32[]{:S(2)}, u32[]{:S(2)}) collective-permute-start(f32[2,16,512]{2,1,0:T(8,128)S(1)} %add_bitcast_fusion.near_ref), channel_id=1, source_target_pairs={{0,16},{1,17},{2,18},{3,19},{4,20},{5,21},{6,22},{7,23},{8,24},{9,... | collective-permute-start | bytes 196616 | tf_op jit(solution)/shard_map/ppermute | solution.py:432
  36.5 0.0 copy-done
  36.5 0.2 fusion.refs_0_
  36.7 1.2 %shard_map.76 = (f32[16,16,512]{2,1,0:T(8,128)S(1)}, f32[16,512]{1,0:T(8,128)S(1)}, f32[3,16,512]{2,1,0:T(8,128)S(1)}, f32[16,16,512]{2,1,0:T(8,128)S(1)}) custom-call(s32[1]{0:T(128)} %bitcast.2.refs_0_, f32[16,8192]{1,0:T(8,128)} %refs_1_.3, f32[16,8192]{1,0:T(8,128)} %refs_2_.3, f32[1,8192]{1,0:T(1,128)} %bitcast.6), custom_call_target="tpu_custom_call" | custom-call | flops 1000000 | bytes 1048576 | tf_op jit(solution)/shard_map/pallas_call | solution.py:437
  37.9 0.0 all-to-all-done
  37.9 2.4 %shard_map.77 = (f32[2,4,256,128]{3,2,1,0:T(8,128)S(1)}, f32[2,4,256,128]{3,2,1,0:T(8,128)S(1)}) custom-call(bf16[2,512,512]{2,1,0:T(8,128)(2,1)S(1)} %fusion.refs_0_, bf16[512,512]{1,0:T(8,128)(2,1)S(1)} %bitcast.5, f32[16,512]{1,0:T(8,128)S(1)} %get-tuple-element.21.refs_2_, f32[3,16,512]{2,1,0:T(8,128)S(1)} %get-tuple-element.22.refs_3_), custom_call_target="tpu_custom_call" | custom-call | flops 25165824 | bytes 2097152 | tf_op jit(solution)/shard_map/pallas_call | solution.py:452
  40.3 0.0 collective-permute-done.5.far_ref
  40.3 1.8 %shard_map.78 = bf16[16,2,16,512]{3,2,1,0:T(8,128)(2,1)S(1)} custom-call(f32[2,16,512]{2,1,0:T(8,128)S(1)} %add_bitcast_fusion.near_ref, f32[2,16,512]{2,1,0:T(8,128)S(1)} %collective-permute-done.5.far_ref, f32[2,4,256,128]{3,2,1,0:T(8,128)S(1)} %get-tuple-element.23.conv_ref, f32[2,4,256,128]{3,2,1,0:T(8,128)S(1)} %get-tuple-element.24.carry_ref, ...), custom_call_target="tpu_custom_call" | custom-call | flops 12582912 | bytes 2097152 | tf_op jit(solution)/shard_map/pallas_call | solution.py:465
  42.1 13.2 %all_to_all.10.mixed_ref = bf16[16,2,16,512]{3,2,1,0:T(8,128)(2,1)S(1)} all-to-all(bf16[16,2,16,512]{3,2,1,0:T(8,128)(2,1)S(1)} %shard_map.78), channel_id=1, replica_groups={{0,1,2,3,4,5,6,7,8,9,10,11,12,13,14,15},{16,17,18,19,20,21,22,23,24,25,..., dimensions={0} | all-to-all | bytes 1048576 | tf_op jit(solution)/shard_map/all_to_all | solution.py:479
  55.3 0.9 %shard_map.79 = bf16[2,16,8192]{2,1,0:T(8,128)(2,1)} custom-call(bf16[16,2,16,512]{3,2,1,0:T(8,128)(2,1)S(1)} %all_to_all.10.mixed_ref), custom_call_target="tpu_custom_call" | custom-call | flops 100000 | bytes 1048576 | tf_op jit(solution)/shard_map/pallas_call | solution.py:480
  (3 shorter events, 0.1 us)
Async XLA Ops:
  0.0 9.7 %collective-permute-start = (bf16[2,32,8192]{2,1,0:T(8,128)(2,1)}, bf16[2,32,8192]{2,1,0:T(8,128)(2,1)S(1)}, u32[]{:S(2)}, u32[]{:S(2)}) collective-permute-start(bf16[2,32,8192]{2,1,0:T(8,128)(2,1)} %refs_2_.2), channel_id=1, source_target_pairs={{0,1},{1,0},{2,3},{3,2},{4,5},{5,4},{6,7},{7,6},{8,9},{9,8},{10,11... | collective-permute-start | bytes 3145736 | tf_op jit(solution)/shard_map/ppermute | solution.py:365
  2.8 35.1 %all-to-all-start = ((bf16[32,16,512]{2,1,0:T(8,128)(2,1)}), bf16[32,16,512]{2,1,0:T(8,128)(2,1)S(1)}, u32[]{:S(2)}, u32[]{:S(2)}) async-start(bf16[32,16,512]{2,1,0:T(8,128)(2,1)} %get-tuple-element.20), calls=%async_computation | async-start | bytes 1048576 | tf_op jit(solution)/shard_map/all_to_all | solution.py:399
  10.5 16.1 %collective-permute-start.1 = (f32[4,2,16,512]{3,2,1,0:T(8,128)S(1)}, f32[4,2,16,512]{3,2,1,0:T(8,128)S(1)}, u32[]{:S(2)}, u32[]{:S(2)}) collective-permute-start(f32[4,2,16,512]{3,2,1,0:T(8,128)S(1)} %shard_map.75), channel_id=1, source_target_pairs={{0,8},{1,9},{2,10},{3,11},{4,12},{5,13},{6,14},{7,15},{8,0},{9,1},... | collective-permute-start | bytes 786440 | tf_op jit(solution)/shard_map/ppermute | solution.py:365
  13.7 22.8 %copy-start = (s32[2,512]{1,0:T(2,128)S(1)}, s32[2,512]{1,0:T(2,128)}, u32[]{:S(2)}) copy-start(s32[2,512]{1,0:T(2,128)} %param.9) | copy-start | bytes 12292
  26.7 5.8 %collective-permute-start.2 = (f32[1,2,16,512]{3,2,1,0:T(8,128)S(1)}, f32[1,2,16,512]{3,2,1,0:T(8,128)S(1)}, u32[]{:S(2)}, u32[]{:S(2)}) collective-permute-start(f32[1,2,16,512]{3,2,1,0:T(8,128)S(1)} %get-tuple-element.27), channel_id=1, source_target_pairs={{0,6},{1,7},{2,4},{3,5},{4,2},{5,3},{6,0},{7,1},{8,14},{9,15},{10,... | collective-permute-start | bytes 196616 | tf_op jit(solution)/shard_map/ppermute | solution.py:365
  29.1 4.3 %collective-permute-start.4 = (f32[1,2,16,512]{3,2,1,0:T(8,128)S(1)}, f32[1,2,16,512]{3,2,1,0:T(8,128)S(1)}, u32[]{:S(2)}, u32[]{:S(2)}) collective-permute-start(f32[1,2,16,512]{3,2,1,0:T(8,128)S(1)} %get-tuple-element.28), channel_id=1, source_target_pairs={{0,2},{1,3},{2,0},{3,1},{4,6},{5,7},{6,4},{7,5},{8,10},{9,11},{10,... | collective-permute-start | bytes 196616 | tf_op jit(solution)/shard_map/ppermute | solution.py:365
  29.7 4.3 %collective-permute-start.3 = (f32[1,2,16,512]{3,2,1,0:T(8,128)S(1)}, f32[1,2,16,512]{3,2,1,0:T(8,128)S(1)}, u32[]{:S(2)}, u32[]{:S(2)}) collective-permute-start(f32[1,2,16,512]{3,2,1,0:T(8,128)S(1)} %get-tuple-element.29), channel_id=1, source_target_pairs={{0,4},{1,5},{2,6},{3,7},{4,0},{5,1},{6,2},{7,3},{8,12},{9,13},{10,... | collective-permute-start | bytes 196616 | tf_op jit(solution)/shard_map/ppermute | solution.py:365
  34.0 6.3 %collective-permute-start.5 = (f32[2,16,512]{2,1,0:T(8,128)S(1)}, f32[2,16,512]{2,1,0:T(8,128)S(1)}, u32[]{:S(2)}, u32[]{:S(2)}) collective-permute-start(f32[2,16,512]{2,1,0:T(8,128)S(1)} %add_bitcast_fusion.near_ref), channel_id=1, source_target_pairs={{0,16},{1,17},{2,18},{3,19},{4,20},{5,21},{6,22},{7,23},{8,24},{9,... | collective-permute-start | bytes 196616 | tf_op jit(solution)/shard_map/ppermute | solution.py:432
